TPU v7x, 256 devices: a whole 4x4x8 slice. The times are simulated.
256 devices in a mesh: wide: 32 (over x, z), narrow: 8 (over y, core).
Axes of the slice: x: 4, y: 4, z: 8, core: 2. Of those that a mesh axis runs over, the one named last changes fastest.
Arguments:
- tile_data: bfloat16 [81920, 128, 128], P(('wide', 'narrow')), may hold values from -0.119628906 to 0.119628906
- tile_user: int32 [81920], P(('wide', 'narrow')), may hold values from 0 to 63
- tile_item: int32 [81920], P(('wide', 'narrow')), may hold values from 0 to 31
- tile_word: int32 [81920], P(('wide', 'narrow')), may hold values from 0 to 4095
- tile_month: int32 [81920], P(('wide', 'narrow')), may hold values from 0 to 999
- tile_live: int32 [256], P(('wide', 'narrow')), may hold values from 160 to 320, as said below
- user_need: int32 [256, 64], P(('wide', 'narrow')), may hold values from 0 to 511, as said below
- item_need: int32 [256, 32], P(('wide', 'narrow')), may hold values from 0 to 511, as said below
- user_slot: int32 [512], replicated, may hold values from 0 to 511, as said below
- item_slot: int32 [512], replicated, may hold values from 0 to 511, as said below
- user_factor: bfloat16 [65536, 128], P('wide'), may hold values from -6 to 6
- word_factor: bfloat16 [4096, 128], replicated, may hold values from -6 to 6
- month_factor: bfloat16 [1000, 128], replicated, may hold values from -6 to 6
Outputs:
- item_rows: float32 [65536, 128], P(('wide', 'narrow'))
Inputs may be any that keep to these rules, and one draw needn't show every extreme that they name: user_slot is a permutation; the owner of user block b is user_slot[b] // 16. item_slot is a permutation; the owner of item block b is item_slot[b] // 16. `user_need`: entries k * 2 to k * 2 + 1 of each row are distinct user blocks whose owner is k. `item_need`: entry k of each row is an item block whose owner is k. `tile_live`: some device has all its slots live.
All inputs are finite; a program needn't handle non-finite values.
Results may differ from a plain program's by a relative error of at most 0.0029.
Values may be sent and summed in bfloat16 or wider, within the bound.
A program may use at most 128 MiB of HBM per device.

v0:
```python
import jax
import jax.numpy as jnp
from jax import lax
from jax.sharding import PartitionSpec as P


def shards(
    tile_data,
    tile_user,
    tile_item,
    tile_word,
    tile_month,
    tile_live,
    user_need,
    item_need,
    user_slot,
    item_slot,
    user_factor,
    word_factor,
    month_factor,
):
    wide_count = lax.axis_size("wide")
    tile_count = tile_data.shape[0]
    block_side = tile_data.shape[1]
    rank_width = user_factor.shape[1]
    items_owned = item_slot.shape[0] // wide_count
    touched = item_need.shape[1]
    item_local = (item_slot[item_need[0]] % items_owned).reshape(wide_count, -1)
    item_from = lax.all_to_all(item_local, "wide", split_axis=0, concat_axis=0, tiled=True)
    user_place = user_slot[user_need[0]]
    gathered = lax.all_gather(user_factor, "wide", axis=0, tiled=True)
    fetched = gathered.reshape(-1, block_side, rank_width)[user_place]
    word_month = word_factor[tile_word].astype(jnp.float32) * month_factor[tile_month].astype(
        jnp.float32
    )
    scaled = (fetched[tile_user].astype(jnp.float32) * word_month[:, None, :]).astype(jnp.bfloat16)
    contrib = jnp.einsum("tab,tar->tbr", tile_data, scaled, preferred_element_type=jnp.float32)
    is_live = lax.iota(jnp.int32, tile_count) < tile_live[0]
    group_ids = jnp.where(is_live, tile_item, touched)
    partial_value = jax.ops.segment_sum(contrib, group_ids, num_segments=touched + 1)[:touched]
    arrived = lax.all_to_all(
        partial_value.reshape(wide_count, -1, block_side, rank_width),
        "wide",
        split_axis=0,
        concat_axis=0,
        tiled=True,
    )
    arrived = arrived.reshape(-1, block_side, rank_width)
    slot_ids = item_from.reshape(-1)
    placing = (slot_ids[:, None] == lax.iota(jnp.int32, items_owned)[None, :]).astype(jnp.float32)
    owner_sum = jnp.einsum("kj,kbr->jbr", placing, arrived, precision=lax.Precision.HIGHEST)
    owned_rows = lax.psum_scatter(owner_sum, "narrow", scatter_dimension=0, tiled=True)
    return owned_rows.reshape(-1, rank_width)


def solution(mesh):
    return jax.shard_map(
        shards,
        mesh=mesh,
        in_specs=(
            P(("wide", "narrow"), None, None),
            P(("wide", "narrow")),
            P(("wide", "narrow")),
            P(("wide", "narrow")),
            P(("wide", "narrow")),
            P(("wide", "narrow")),
            P(("wide", "narrow"), None),
            P(("wide", "narrow"), None),
            P(),
            P(),
            P("wide", None),
            P(),
            P(),
        ),
        out_specs=P(("wide", "narrow"), None),
        check_vma=False,
    )
```

profile of v0, /device:TPU:4, one launch (start us, length us, event | category | flops | bytes accessed | tf_op | source)
XLA Modules:
  0.0 346.2 jit_solution(6248891772234273754)
XLA Ops:
  6.5 0.0 all-gather.2.cloned.1.call-start
  6.5 0.7 all-gather.2.cloned.1.call-update
  7.3 0.7 fusion.11
  7.9 1.4 gather_fusion
  9.3 0.7 copy.26
  10.0 11.6 %all-to-all-start = ((s32[32,1,1]{2,1,0:T(1,128)}), s32[32,1,1]{2,1,0:T(1,128)S(1)}, u32[]{:S(2)}, u32[]{:S(2)}) async-start(s32[32,1,1]{2,1,0:T(1,128)} %copy.26), calls=%async_computation | async-start | bytes 32768 | tf_op jit(solution)/shard_map/all_to_all | solution.py:29
  22.3 0.7 fusion.12
  22.9 1.5 gather_fusion.1
  24.4 0.7 compare_select_fusion.1
  25.1 1.4 gather_fusion.4
  26.5 0.7 compare_select_fusion
  27.2 2.1 gather_fusion.5
  29.4 0.7 compare_select_fusion.2
  30.1 0.7 fusion.9
  30.8 121.1 %all-gather.2.cloned.1.call-done = bf16[65536,128]{1,0:T(8,128)(2,1)} async-done(((bf16[2048,128]{1,0:T(8,128)(2,1)}), bf16[65536,128]{1,0:T(8,128)(2,1)}) %all-gather.2.cloned.1.call-update) | async-done | bytes 16777232 | tf_op jit(solution)/shard_map/all_gather | solution.py:31
  151.9 6.7 %gather_fusion.2 = bf16[64,128,128]{2,1,0:T(8,128)(2,1)S(1)} fusion(bf16[512,128,128]{2,1,0:T(8,128)(2,1)} %bitcast.31, s32[1024]{0:T(1024)S(1)} %pad_clamp_fusion.3), kind=kCustom, calls=%fused_computation.2 | custom fusion | bytes 4194560 | tf_op jit(solution)/shard_map/gather | solution.py:32
  158.6 10.7 %gather_fusion.3 = bf16[320,128,128]{2,1,0:T(8,128)(2,1)} fusion(bf16[64,128,128]{2,1,0:T(8,128)(2,1)S(1)} %gather_fusion.2, s32[1024]{0:T(1024)S(1)} %pad_clamp_fusion.2), kind=kCustom, calls=%fused_computation.3 | custom fusion | bytes 20972800 | tf_op jit(solution)/shard_map/gather | solution.py:36
  169.3 12.9 %fusion.2 = f32[320,128,128]{1,2,0:T(8,128)} fusion(bf16[320,128,128]{2,1,0:T(8,128)(2,1)} %param.13, bf16[320,128,128]{2,1,0:T(8,128)(2,1)} %gather_fusion.3, f32[320,128]{1,0:T(8,128)S(1)} %convert_multiply_fusion), kind=kOutput, calls=%fused_computation.10 | convolution fusion | flops 1357905920 | bytes 42106880 | tf_op jit(solution)/shard_map/tab,tar->tbr/dot_general | solution.py:37
  182.3 21.1 %copy.28 = f32[320,128,128]{2,1,0:T(8,128)} copy(f32[320,128,128]{1,2,0:T(8,128)} %fusion.2) | data formatting | bytes 41943040 | tf_op jit(solution)/shard_map/tab,tar->tbr/dot_general | solution.py:37
  203.4 0.2 broadcast_in_dim.24
  203.7 0.0 copy-start.1
  203.7 41.9 %scatter_fusion = f32[33,128,128]{2,1,0:T(8,128)S(1)} fusion(f32[33,128,128]{2,1,0:T(8,128)S(1)} %broadcast_in_dim.24, s32[320]{0:T(512)S(1)} %fusion.9, f32[320,128,128]{2,1,0:T(8,128)} %copy.28), kind=kCustom, calls=%fused_computation.6 | custom fusion | flops 5242880 | bytes 62915840 | tf_op jit(solution)/shard_map/scatter-add | solution.py:40
  245.6 1.5 slice_bitcast_fusion
  247.1 0.0 all-to-all-done
  247.1 7.5 %all-to-all-start.1 = ((f32[32,1,128,128]{3,2,1,0:T(8,128)}), f32[32,1,128,128]{3,2,1,0:T(8,128)S(1)}, u32[]{:S(2)}, u32[]{:S(2)}) async-start(f32[32,1,128,128]{3,2,1,0:T(8,128)} %slice_bitcast_fusion), calls=%async_computation.1 | async-start | bytes 4194304 | tf_op jit(solution)/shard_map/all_to_all | solution.py:41
  254.5 0.0 reduce-scatter.2.cloned.1.call-start
  254.6 0.7 reduce
  255.2 46.4 %all-to-all-done.1 = f32[32,1,128,128]{3,2,1,0:T(8,128)S(1)} async-done(((f32[32,1,128,128]{3,2,1,0:T(8,128)}), f32[32,1,128,128]{3,2,1,0:T(8,128)S(1)}, u32[]{:S(2)}, u32[]{:S(2)}) %all-to-all-start.1) | async-done | bytes 2097184 | tf_op jit(solution)/shard_map/all_to_all | solution.py:41
  301.7 2.0 fusion.3
  303.7 1.3 copy.31
  305.0 0.0 reduce-scatter.2.cloned.1.call-update
  305.0 34.4 %reduce-scatter.2.cloned.1.call-done = f32[2,128,128]{2,1,0:T(8,128)} async-done(((f32[16,128,128]{2,1,0:T(8,128)}), f32[2,128,128]{2,1,0:T(8,128)}) %reduce-scatter.2.cloned.1.call-update) | async-done | bytes 131088 | tf_op jit(solution)/shard_map/reduce_scatter | solution.py:52
  (12 shorter events, 0.1 us)
Async XLA Ops:
  6.5 18.6 %copy-start = (bf16[4096,128]{1,0:T(8,128)(2,1)S(1)}, bf16[4096,128]{1,0:T(8,128)(2,1)}, u32[]{:S(2)}) copy-start(bf16[4096,128]{1,0:T(8,128)(2,1)} %param.24) | copy-start | bytes 3145732
  6.5 145.3 %all-gather.2.cloned.1.call-start = ((), (), s32[]{:S(2)}) async-start(), calls=%async_computation.3 | async-start | bytes 17301504 | tf_op jit(solution)/shard_map/all_gather | solution.py:31
  10.0 237.0 %all-to-all-start = ((s32[32,1,1]{2,1,0:T(1,128)}), s32[32,1,1]{2,1,0:T(1,128)S(1)}, u32[]{:S(2)}, u32[]{:S(2)}) async-start(s32[32,1,1]{2,1,0:T(1,128)} %copy.26), calls=%async_computation | async-start | bytes 32768 | tf_op jit(solution)/shard_map/all_to_all | solution.py:29
  203.7 135.7 %copy-start.1 = (bf16[4096,128]{1,0:T(8,128)(2,1)S(1)}, bf16[4096,128]{1,0:T(8,128)(2,1)}, u32[]{:S(2)}) copy-start(bf16[4096,128]{1,0:T(8,128)(2,1)} %param.24) | copy-start | bytes 3145732
  247.1 54.6 %all-to-all-start.1 = ((f32[32,1,128,128]{3,2,1,0:T(8,128)}), f32[32,1,128,128]{3,2,1,0:T(8,128)S(1)}, u32[]{:S(2)}, u32[]{:S(2)}) async-start(f32[32,1,128,128]{3,2,1,0:T(8,128)} %slice_bitcast_fusion), calls=%async_computation.1 | async-start | bytes 4194304 | tf_op jit(solution)/shard_map/all_to_all | solution.py:41
  254.5 84.8 %reduce-scatter.2.cloned.1.call-start = ((), (), s32[]{:S(2)}) async-start(), calls=%async_computation.4 | async-start | bytes 1179648 | tf_op jit(solution)/shard_map/reduce_scatter | solution.py:52
Sparse Core Ops, SparseCore 0:
  10.0 141.8 all-gather.1
  305.1 34.2 reduce-scatter.1
where the time goes:
time: 348 us; the launch traced here: 346 us
  waiting for transfers between devices  203 us (58%)
  local copies, waits for them, and re-layouts  48.7 us (14%)
  other arithmetic  46.7 us (13%)
  starting transfers between devices  19.1 us (5%)
  matrix products  14.9 us (4%)
  between operations  14.1 us (4%)
    all_gather x1, waiting for transfers between devices, shards(): gathered = lax.all_gather(user_factor, 'wide', axis=0, tiled=True)  121 us
    all_to_all x1, waiting for transfers between devices, shards(): lax.all_to_all(partial_value.reshape(wide_count, -1, block_side, rank_wid...  46.4 us
    scatter-add x1, other arithmetic, shards(): jax.ops.segment_sum(contrib, group_ids, num_segments=touched + 1)[:touched]  41.9 us
    reduce_scatter x1, waiting for transfers between devices, shards(): lax.psum_scatter(owner_sum, 'narrow', scatter_dimension=0, tiled=True)  34.4 us
    dot_general x1, local copies, waits for them, and re-layouts, shards(): jnp.einsum('tab,tar->tbr', tile_data, scaled, preferred_element_type=jnp....  21.1 us
    dot_general x1, matrix products, shards(): jnp.einsum('tab,tar->tbr', tile_data, scaled, preferred_element_type=jnp....  12.9 us
    all_to_all x1, starting transfers between devices, shards(): lax.all_to_all(item_local, 'wide', split_axis=0, concat_axis=0, tiled=True)  11.6 us
    gather x1, local copies, waits for them, and re-layouts, shards(): fetched[tile_user].astype(jnp.float32) * word_month[:, None, :]  10.7 us
  transfers between devices with their start and end apart: 4, of which 3 were waited for; matrix products, arithmetic and copies ran while one was open for 31% of the time, Pallas kernels for 0%

commit v1 on v0

--- a/solution.py
+++ b/solution.py
@@ -28,7 +28,9 @@
     item_local = (item_slot[item_need[0]] % items_owned).reshape(wide_count, -1)
     item_from = lax.all_to_all(item_local, "wide", split_axis=0, concat_axis=0, tiled=True)
     user_place = user_slot[user_need[0]]
-    gathered = lax.all_gather(user_factor, "wide", axis=0, tiled=True)
+    gathered = jnp.concatenate(
+        lax.all_to_all(jnp.stack([user_factor] * lax.axis_size("wide")), "wide", 0, 0), axis=0
+    )
     fetched = gathered.reshape(-1, block_side, rank_width)[user_place]
     word_month = word_factor[tile_word].astype(jnp.float32) * month_factor[tile_month].astype(
         jnp.float32

time: 348 us -> 639 us (1.84)
  waiting for transfers between devices: 203 us -> 457 us
  starting transfers between devices: 19.1 us -> 55.1 us
    all_to_all x0 -> x1, waiting for transfers between devices: none -> 377 us  [shards(): lax.all_to_all(jnp.stack([user_factor] * lax.axis_size('wide')), 'wide',...]
    all_gather x1 -> x0, waiting for transfers between devices: 121 us -> none  [shards(): gathered = lax.all_gather(user_factor, 'wide', axis=0, tiled=True)]
    all_to_all x1, starting transfers between devices: 11.6 us -> 33.3 us  [shards(): lax.all_to_all(item_local, 'wide', split_axis=0, concat_axis=0, tiled=True)]
    all_to_all x0 -> x1, starting transfers between devices: none -> 11.8 us  [shards(): lax.all_to_all(jnp.stack([user_factor] * lax.axis_size('wide')), 'wide',...]
    another operation x0 -> x1, local copies, waits for them, and re-layouts: none -> 7.07 us  [shards(): jnp.stack([user_factor] * lax.axis_size('wide'))]
  transfers between devices with their start and end apart: 4 -> 4, of which waited for: 3 -> 3; matrix products, arithmetic and copies ran while one was open for 31% -> 16% of each run, Pallas kernels for 0% -> 0%
where the time goes in v1:
time: 639 us; the launch traced here: 637 us
  waiting for transfers between devices  457 us (72%)
  starting transfers between devices  55.1 us (9%)
  local copies, waits for them, and re-layouts  53.7 us (8%)
  other arithmetic  42.7 us (7%)
  matrix products  14.9 us (2%)
  between operations  14.3 us (2%)
    all_to_all x1, waiting for transfers between devices, shards(): lax.all_to_all(jnp.stack([user_factor] * lax.axis_size('wide')), 'wide',...  377 us
    all_to_all x1, waiting for transfers between devices, shards(): lax.all_to_all(partial_value.reshape(wide_count, -1, block_side, rank_wid...  45.4 us
    scatter-add x1, other arithmetic, shards(): jax.ops.segment_sum(contrib, group_ids, num_segments=touched + 1)[:touched]  41.9 us
    reduce_scatter x1, waiting for transfers between devices, shards(): lax.psum_scatter(owner_sum, 'narrow', scatter_dimension=0, tiled=True)  34.1 us
    all_to_all x1, starting transfers between devices, shards(): lax.all_to_all(item_local, 'wide', split_axis=0, concat_axis=0, tiled=True)  33.3 us
    dot_general x1, local copies, waits for them, and re-layouts, shards(): jnp.einsum('tab,tar->tbr', tile_data, scaled, preferred_element_type=jnp....  21.1 us
    dot_general x1, matrix products, shards(): jnp.einsum('tab,tar->tbr', tile_data, scaled, preferred_element_type=jnp....  12.9 us
  transfers between devices with their start and end apart: 4, of which 3 were waited for; matrix products, arithmetic and copies ran while one was open for 16% of the time, Pallas kernels for 0%

profile of v1, /device:TPU:4, one launch (start us, length us, event | category | flops | bytes accessed | tf_op | source)
XLA Modules:
  0.0 637.3 jit_solution(7277944701398943559)
XLA Ops:
  6.5 7.1 %stack.2 = bf16[32,2048,128]{2,1,0:T(8,128)(2,1)} broadcast(bf16[2048,128]{1,0:T(8,128)(2,1)} %param.23), dimensions={1,2} | broadcast | bytes 17301504 | tf_op jit(solution)/shard_map/stack | solution.py:32
  13.6 0.0 copy-start.3
  13.6 0.0 copy-start.5
  13.6 0.0 copy-start.6
  13.7 0.0 copy-start.4
  13.7 0.0 copy-start.7
  13.7 0.0 copy-start.8
  13.7 11.8 %all-to-all-start.1 = ((bf16[32,2048,128]{2,1,0:T(8,128)(2,1)}), bf16[32,2048,128]{2,1,0:T(8,128)(2,1)}, u32[]{:S(2)}, u32[]{:S(2)}) async-start(bf16[32,2048,128]{2,1,0:T(8,128)(2,1)} %stack.2), calls=%async_computation.1 | async-start | bytes 33554432 | tf_op jit(solution)/shard_map/all_to_all | solution.py:32
  26.2 0.7 gather_fusion
  26.9 0.7 copy.26
  27.6 0.8 gather_fusion.1
  28.5 1.4 gather_fusion.4
  29.9 1.4 gather_fusion.5
  31.4 377.0 %all-to-all-done.1 = bf16[32,2048,128]{2,1,0:T(8,128)(2,1)} async-done(((bf16[32,2048,128]{2,1,0:T(8,128)(2,1)}), bf16[32,2048,128]{2,1,0:T(8,128)(2,1)}, u32[]{:S(2)}, u32[]{:S(2)}) %all-to-all-start.1) | async-done | bytes 16777248 | tf_op jit(solution)/shard_map/all_to_all | solution.py:32
  408.4 33.3 %all-to-all-start = ((s32[32,1,1]{2,1,0:T(1,128)}), s32[32,1,1]{2,1,0:T(1,128)S(1)}, u32[]{:S(2)}, u32[]{:S(2)}) async-start(s32[32,1,1]{2,1,0:T(1,128)} %copy.26), calls=%async_computation | async-start | bytes 32768 | tf_op jit(solution)/shard_map/all_to_all | solution.py:29
  441.8 6.7 %gather_fusion.2 = bf16[64,128,128]{2,1,0:T(8,128)(2,1)S(1)} fusion(bf16[512,128,128]{2,1,0:T(8,128)(2,1)} %bitcast.5, s32[1024]{0:T(1024)S(1)} %pad_clamp_fusion.3), kind=kCustom, calls=%fused_computation.2 | custom fusion | bytes 4194560 | tf_op jit(solution)/shard_map/gather | solution.py:34
  448.5 10.7 %gather_fusion.3 = bf16[320,128,128]{2,1,0:T(8,128)(2,1)} fusion(bf16[64,128,128]{2,1,0:T(8,128)(2,1)S(1)} %gather_fusion.2, s32[1024]{0:T(1024)S(1)} %pad_clamp_fusion.2), kind=kCustom, calls=%fused_computation.3 | custom fusion | bytes 20972800 | tf_op jit(solution)/shard_map/gather | solution.py:38
  459.2 12.9 %fusion.2 = f32[320,128,128]{1,2,0:T(8,128)} fusion(bf16[320,128,128]{2,1,0:T(8,128)(2,1)} %param.13, bf16[320,128,128]{2,1,0:T(8,128)(2,1)} %gather_fusion.3, f32[320,128]{1,0:T(8,128)S(1)} %convert_multiply_fusion), kind=kOutput, calls=%fused_computation.10 | convolution fusion | flops 1357905920 | bytes 42106880 | tf_op jit(solution)/shard_map/tab,tar->tbr/dot_general | solution.py:39
  472.2 21.1 %copy.28 = f32[320,128,128]{2,1,0:T(8,128)} copy(f32[320,128,128]{1,2,0:T(8,128)} %fusion.2) | data formatting | bytes 41943040 | tf_op jit(solution)/shard_map/tab,tar->tbr/dot_general | solution.py:39
  493.3 0.2 broadcast_in_dim.24
  493.6 0.0 copy-start.1
  493.6 41.9 %scatter_fusion = f32[33,128,128]{2,1,0:T(8,128)S(1)} fusion(f32[33,128,128]{2,1,0:T(8,128)S(1)} %broadcast_in_dim.24, s32[320]{0:T(512)S(1)} %fusion.9, f32[320,128,128]{2,1,0:T(8,128)} %copy.28), kind=kCustom, calls=%fused_computation.6 | custom fusion | flops 5242880 | bytes 62915840 | tf_op jit(solution)/shard_map/scatter-add | solution.py:42
  535.5 1.5 slice_bitcast_fusion
  537.0 0.0 all-to-all-done
  537.0 9.8 %all-to-all-start.2 = ((f32[32,1,128,128]{3,2,1,0:T(8,128)}), f32[32,1,128,128]{3,2,1,0:T(8,128)S(1)}, u32[]{:S(2)}, u32[]{:S(2)}) async-start(f32[32,1,128,128]{3,2,1,0:T(8,128)} %slice_bitcast_fusion), calls=%async_computation.2 | async-start | bytes 4194304 | tf_op jit(solution)/shard_map/all_to_all | solution.py:43
  546.7 0.2 reduce-scatter.2.cloned.1.call-start
  547.0 0.7 reduce
  547.6 45.4 %all-to-all-done.2 = f32[32,1,128,128]{3,2,1,0:T(8,128)S(1)} async-done(((f32[32,1,128,128]{3,2,1,0:T(8,128)}), f32[32,1,128,128]{3,2,1,0:T(8,128)S(1)}, u32[]{:S(2)}, u32[]{:S(2)}) %all-to-all-start.2) | async-done | bytes 2097184 | tf_op jit(solution)/shard_map/all_to_all | solution.py:43
  593.0 2.0 fusion.3
  595.0 1.3 copy.31
  596.3 0.0 reduce-scatter.2.cloned.1.call-update
  596.4 34.1 %reduce-scatter.2.cloned.1.call-done = f32[2,128,128]{2,1,0:T(8,128)} async-done(((f32[16,128,128]{2,1,0:T(8,128)}), f32[2,128,128]{2,1,0:T(8,128)}) %reduce-scatter.2.cloned.1.call-update) | async-done | bytes 131088 | tf_op jit(solution)/shard_map/reduce_scatter | solution.py:54
  (30 shorter events, 0.1 us)
Async XLA Ops:
  6.5 21.9 %copy-start = (bf16[4096,128]{1,0:T(8,128)(2,1)S(1)}, bf16[4096,128]{1,0:T(8,128)(2,1)}, u32[]{:S(2)}) copy-start(bf16[4096,128]{1,0:T(8,128)(2,1)} %param.24) | copy-start | bytes 3145732
  13.6 12.5 %copy-start.9 = (s32[1,32]{1,0:T(1,128)S(1)}, s32[1,32]{1,0:T(1,128)}, u32[]{:S(2)}) copy-start(s32[1,32]{1,0:T(1,128)} %param.20) | copy-start | bytes 388
  13.6 12.6 %copy-start.2 = (s32[512]{0:T(512)S(1)}, s32[512]{0:T(512)}, u32[]{:S(2)}) copy-start(s32[512]{0:T(512)} %param.22) | copy-start | bytes 6148
  13.6 14.0 %copy-start.10 = (s32[1,64]{1,0:T(1,128)S(1)}, s32[1,64]{1,0:T(1,128)}, u32[]{:S(2)}) copy-start(s32[1,64]{1,0:T(1,128)} %param.19) | copy-start | bytes 772
  13.6 14.0 %copy-start.3 = (s32[512]{0:T(512)S(1)}, s32[512]{0:T(512)}, u32[]{:S(2)}) copy-start(s32[512]{0:T(512)} %param.21) | copy-start | bytes 6148
  13.6 14.8 %copy-start.5 = (s32[320]{0:T(512)S(1)}, s32[320]{0:T(512)}, u32[]{:S(2)}) copy-start(s32[320]{0:T(512)} %param.16) | copy-start | bytes 3844
  13.6 16.2 %copy-start.6 = (s32[320]{0:T(512)S(1)}, s32[320]{0:T(512)}, u32[]{:S(2)}) copy-start(s32[320]{0:T(512)} %param.17) | copy-start | bytes 3844
  13.7 16.3 %copy-start.4 = (bf16[1000,128]{1,0:T(8,128)(2,1)S(1)}, bf16[1000,128]{1,0:T(8,128)(2,1)}, u32[]{:S(2)}) copy-start(bf16[1000,128]{1,0:T(8,128)(2,1)} %param.25) | copy-start | bytes 768004
  13.7 17.7 %copy-start.7 = (s32[320]{0:T(512)S(1)}, s32[320]{0:T(512)}, u32[]{:S(2)}) copy-start(s32[320]{0:T(512)} %param.14) | copy-start | bytes 3844
  13.7 17.7 %copy-start.8 = (s32[320]{0:T(512)S(1)}, s32[320]{0:T(512)}, u32[]{:S(2)}) copy-start(s32[320]{0:T(512)} %param.15) | copy-start | bytes 3844
  13.7 394.7 %all-to-all-start.1 = ((bf16[32,2048,128]{2,1,0:T(8,128)(2,1)}), bf16[32,2048,128]{2,1,0:T(8,128)(2,1)}, u32[]{:S(2)}, u32[]{:S(2)}) async-start(bf16[32,2048,128]{2,1,0:T(8,128)(2,1)} %stack.2), calls=%async_computation.1 | async-start | bytes 33554432 | tf_op jit(solution)/shard_map/all_to_all | solution.py:32
  408.4 128.5 %all-to-all-start = ((s32[32,1,1]{2,1,0:T(1,128)}), s32[32,1,1]{2,1,0:T(1,128)S(1)}, u32[]{:S(2)}, u32[]{:S(2)}) async-start(s32[32,1,1]{2,1,0:T(1,128)} %copy.26), calls=%async_computation | async-start | bytes 32768 | tf_op jit(solution)/shard_map/all_to_all | solution.py:29
  493.6 136.9 %copy-start.1 = (bf16[4096,128]{1,0:T(8,128)(2,1)S(1)}, bf16[4096,128]{1,0:T(8,128)(2,1)}, u32[]{:S(2)}) copy-start(bf16[4096,128]{1,0:T(8,128)(2,1)} %param.24) | copy-start | bytes 3145732
  537.0 56.1 %all-to-all-start.2 = ((f32[32,1,128,128]{3,2,1,0:T(8,128)}), f32[32,1,128,128]{3,2,1,0:T(8,128)S(1)}, u32[]{:S(2)}, u32[]{:S(2)}) async-start(f32[32,1,128,128]{3,2,1,0:T(8,128)} %slice_bitcast_fusion), calls=%async_computation.2 | async-start | bytes 4194304 | tf_op jit(solution)/shard_map/all_to_all | solution.py:43
  546.7 83.7 %reduce-scatter.2.cloned.1.call-start = ((), (), s32[]{:S(2)}) async-start(), calls=%async_computation.4 | async-start | bytes 1179648 | tf_op jit(solution)/shard_map/reduce_scatter | solution.py:54
Sparse Core Ops, SparseCore 0:
  596.5 33.9 reduce-scatter.1
